TPU v7x, 256 devices: a whole 4x4x8 slice. The times are simulated.
256 devices in a mesh: seq: 16 (over y_hi, z), batch: 16 (over y_lo, x, core).
Axes of the slice: x: 4, y: 4 (y_hi: 2, y_lo: 2; y = y_hi * 2 + y_lo), z: 8, core: 2. Of those that a mesh axis runs over, the one named last changes fastest.
Arguments:
- tokens: bfloat16 [16, 8192, 1536], P('batch', 'seq'), may hold values from -24 to 24
- filter_tap_weight: float32 [5, 1536], replicated, may hold values from -2.4 to 2.4
- norm_gain: float32 [1536], replicated, may hold values from 0.5 to 1.5
- query_weight: bfloat16 [1536, 512], replicated, may hold values from -4 to 4
- keyval_weight: bfloat16 [1536, 320], replicated, may hold values from -1 to 1
- head_weight: bfloat16 [768, 2, 384], replicated, may hold values from -0.21875 to 0.21875
- head_bias: float32 [2, 384], replicated, may hold values from -1 to 1
- exon_start: int32 [16, 32, 8], P('batch'), may hold values from 0 to 8191, as said below
- exon_end: int32 [16, 32, 8], P('batch'), may hold values from 0 to 8192, as said below
- gene_strand: int32 [16, 32], P('batch'), may hold values from 0 to 1
- gene_owner: int32 [16, 32, 1], P('batch'), may hold values from 0 to 15; in each aligned block of 32 rows (0 to 31, 32 to 63, ..., all dimensions but the last counted through in order) at most 4 rows name the same one
- gene_target: float32 [16, 16, 4, 384], P('batch'), may hold values from 0 to 4
Outputs:
- coverage: bfloat16 [16, 8192, 2, 384], P('batch', 'seq')
- gene_pred: float32 [16, 16, 4, 384], P('batch')
- head_grad: float32 [768, 2, 384], replicated
- bias_grad: float32 [2, 384], replicated
Inputs may be any that keep to these rules, and one draw needn't show every extreme that they name: `exon_start`: exons of a gene lie inside the window in increasing order without intersection, each of 1 to 4 bins; unused exon slots have start equal to end; every gene has at least one exon. `exon_end`: as exon_start. `gene_owner`: at most 4 genes of one window have the same owner.
All inputs are finite; a program needn't handle non-finite values.
Results may differ from a plain program's by a relative error of at most 0.025.
Values may be sent and summed in bfloat16 or wider, within the bound.
No kernel may reach another device: no remote copies, remote signals or barrier semaphores. Data moves between devices by JAX's collectives and lax.ppermute only.
A program may use at most 64 MiB of HBM per device.

v0:
```python
import math
import jax
import jax.numpy as jnp
from jax import lax
from jax.sharding import PartitionSpec as P

HEADS = 4
DK = 128
DV = 192
TRK = 384
FILTER_TAP_COUNT = 5
DILATION_STRIDE = 64


def extended(block, sides, width):
    for axis, dim in sides:
        count = lax.axis_size(axis)
        forward = [(i, i + 1) for i in range(count - 1)]
        backward = [(target, source) for source, target in forward]
        low = lax.ppermute(
            lax.slice_in_dim(block, block.shape[dim] - width, None, axis=dim), axis, forward
        )
        high = lax.ppermute(lax.slice_in_dim(block, 0, width, axis=dim), axis, backward)
        block = jnp.concatenate([low, block, high], axis=dim)
    return block


def make_fold(query_rows, scale_factor, state_now, pieces):
    key_rows, value_rows = pieces
    key_count = key_rows.shape[0]
    block_rows = math.gcd(key_count, 512)
    block_count = key_count // block_rows
    key_blocks = key_rows.reshape(block_count, block_rows, key_rows.shape[1])
    value_blocks = value_rows.reshape(block_count, block_rows, value_rows.shape[1])

    def one_block(running, block_pair):
        running_max, running_sum, weighted = running
        key_block, value_block = block_pair
        scores = (
            jnp.einsum("qhd,kd->qhk", query_rows, key_block, preferred_element_type=jnp.float32)
            * scale_factor
        )
        new_max = jnp.maximum(running_max, jnp.max(scores, axis=-1))
        shrink = jnp.exp(running_max - new_max)
        weights = jnp.exp(scores - new_max[..., None])
        running_sum = running_sum * shrink + jnp.sum(weights, axis=-1)
        weighted = weighted * shrink[..., None] + jnp.einsum(
            "qhk,kd->qhd",
            weights.astype(jnp.bfloat16),
            value_block,
            preferred_element_type=jnp.float32,
        )
        return ((new_max, running_sum, weighted), None)

    result_state, unused = lax.scan(one_block, state_now, (key_blocks, value_blocks))
    return result_state


def local(
    tokens,
    filter_tap_weight,
    norm_gain,
    query_weight,
    keyval_weight,
    head_weight,
    head_bias,
    exon_start,
    exon_end,
    gene_strand,
    gene_owner,
    gene_target,
):
    local_rows = tokens[0]
    window_row_count = local_rows.shape[0]
    dilation_reach_rows = FILTER_TAP_COUNT // 2 * DILATION_STRIDE
    zero_extended = extended(local_rows, (("seq", 0),), dilation_reach_rows)
    tap_total = local_rows.astype(jnp.float32)
    for filter_tap_index in range(FILTER_TAP_COUNT):
        tap_total = tap_total + filter_tap_weight[filter_tap_index] * zero_extended[
            filter_tap_index * DILATION_STRIDE : filter_tap_index * DILATION_STRIDE
            + window_row_count
        ].astype(jnp.float32)
    spread = jnp.mean(tap_total * tap_total, axis=-1, keepdims=True)
    normed = (tap_total * lax.rsqrt(spread + 1e-06) * norm_gain).astype(jnp.bfloat16)
    queries = jnp.dot(normed, query_weight, preferred_element_type=jnp.float32).astype(jnp.bfloat16)
    keyval = jnp.dot(normed, keyval_weight, preferred_element_type=jnp.float32)
    key_rows = keyval[:, :DK].astype(jnp.bfloat16)
    value_rows = keyval[:, DK:].astype(jnp.bfloat16)
    query_rows = queries.reshape(window_row_count, HEADS, DK)
    start_state = (
        jnp.full((window_row_count, HEADS), -jnp.inf, jnp.float32),
        jnp.zeros((window_row_count, HEADS), jnp.float32),
        jnp.zeros((window_row_count, HEADS, DV), jnp.float32),
    )
    running_max, running_sum, weighted = make_fold(
        query_rows,
        DK ** (-0.5),
        start_state,
        (
            lax.all_gather(key_rows, "seq", axis=0, tiled=True),
            lax.all_gather(value_rows, "seq", axis=0, tiled=True),
        ),
    )
    hidden_width = HEADS * DV
    attended = (
        (weighted / running_sum[..., None])
        .reshape(window_row_count, hidden_width)
        .astype(jnp.bfloat16)
    )
    logits = jnp.dot(
        attended, head_weight.reshape(hidden_width, 2 * TRK), preferred_element_type=jnp.float32
    ) + head_bias.reshape(2 * TRK)
    coverage = jax.nn.softplus(logits).astype(jnp.bfloat16).reshape(1, window_row_count, 2, TRK)
    positions = lax.axis_index("seq") * window_row_count + jnp.arange(
        window_row_count, dtype=jnp.int32
    )
    starts = exon_start[0]
    exon_stops = exon_end[0]
    inside = (positions[None, None, :] >= starts[:, :, None]) & (
        positions[None, None, :] < exon_stops[:, :, None]
    )
    counts = jnp.sum(inside.astype(jnp.int32), axis=1).astype(jnp.bfloat16)
    partial_pool = jnp.dot(counts, attended, preferred_element_type=jnp.float32)
    pooled = lax.psum(partial_pool.astype(jnp.bfloat16), "seq").astype(jnp.float32)
    length = jnp.sum((exon_stops - starts).astype(jnp.float32), axis=1)
    pooled = pooled / length[:, None]
    track_share = TRK
    weight_part = head_weight.astype(jnp.float32)
    per_strand = (
        jnp.einsum("gh,hst->gst", pooled, weight_part, precision=lax.Precision.HIGHEST)
        + head_bias[None]
    )
    strands = gene_strand[0]
    gene_logit = jnp.where(strands[:, None] == 0, per_strand[:, 0], per_strand[:, 1])
    owners = gene_owner[0, :, 0]
    gene_index = jnp.arange(owners.shape[0], dtype=jnp.int32)
    earlier = (owners[:, None] == owners[None, :]) & (gene_index[None, :] < gene_index[:, None])
    slot_rank = jnp.sum(earlier.astype(jnp.int32), axis=1)
    capacity = gene_target.shape[2]
    owner_count = lax.axis_size("batch")
    slot_index = owners * capacity + slot_rank
    slot_table = (
        jnp.arange(owner_count * capacity, dtype=jnp.int32)[:, None] == slot_index[None, :]
    ).astype(jnp.float32)
    outgoing = jnp.dot(
        slot_table, jax.nn.softplus(gene_logit), precision=lax.Precision.HIGHEST
    ).reshape(owner_count, capacity, track_share)
    arrived = lax.all_to_all(
        outgoing.astype(jnp.bfloat16), "batch", split_axis=0, concat_axis=0, tiled=True
    ).astype(outgoing.dtype)
    target_part = gene_target[0]
    gene_slope = (jnp.log1p(arrived) - target_part) / (1.0 + arrived)
    returned = lax.all_to_all(
        gene_slope.astype(jnp.bfloat16), "batch", split_axis=0, concat_axis=0, tiled=True
    ).astype(gene_slope.dtype)
    slope_rows = jnp.dot(
        slot_table.T,
        returned.reshape(owner_count * capacity, track_share),
        precision=lax.Precision.HIGHEST,
    )
    logit_grad = slope_rows * jax.nn.sigmoid(gene_logit)
    placed = jnp.stack(
        [
            jnp.where(strands[:, None] == 0, logit_grad, 0.0),
            jnp.where(strands[:, None] == 1, logit_grad, 0.0),
        ],
        axis=1,
    )
    window_head = jnp.einsum("gh,gst->hst", pooled, placed, precision=lax.Precision.HIGHEST)
    window_bias = jnp.sum(placed, axis=0)
    head_grad, bias_grad = (
        lax.psum(window_head.astype(jnp.bfloat16), "batch").astype(jnp.float32),
        lax.psum(window_bias.astype(jnp.bfloat16), "batch").astype(jnp.float32),
    )
    return (coverage, arrived[None], head_grad, bias_grad)


def solution(mesh):
    in_specs = (
        P("batch", "seq", None),
        P(),
        P(),
        P(),
        P(),
        P(),
        P(),
        P("batch", None, None),
        P("batch", None, None),
        P("batch", None),
        P("batch", None, None),
        P("batch", None, None, None),
    )
    out_specs = (P("batch", "seq", None, None), P("batch", None, None, None), P(), P())
    return jax.shard_map(local, mesh=mesh, in_specs=in_specs, out_specs=out_specs, check_vma=False)
```

profile of v0, /device:TPU:1, one launch (start us, length us, event | category | flops | bytes accessed | tf_op | source)
XLA Modules:
  0.0 601.8 jit_solution(12786762936528325310)
XLA Ops:
  8.6 4.4 collective-permute-start
  15.4 5.3 collective-permute-done
  20.7 4.2 collective-permute-done.1
  32.8 3.8 convolution_convert_fusion.1
  38.7 77.2 %all-gather.3.cloned.1.call-done = bf16[8192,128]{0,1:T(8,128)(2,1)} async-done(((bf16[512,128]{0,1:T(8,128)(2,1)}), bf16[8192,128]{0,1:T(8,128)(2,1)}) %all-gather.3.cloned.1.call-update) | async-done | bytes 2097168 | tf_op jit(solution)/shard_map/all_gather | solution.py:100
  115.9 4.1 copy.56
  120.0 90.2 %all-gather.5.cloned.1.call-done = bf16[8192,192]{0,1:T(8,128)(2,1)} async-done(((bf16[512,192]{0,1:T(8,128)(2,1)}), bf16[8192,192]{0,1:T(8,128)(2,1)}) %all-gather.5.cloned.1.call-update) | async-done | bytes 3145744 | tf_op jit(solution)/shard_map/all_gather | solution.py:101
  210.1 3.9 copy.64
  214.0 151.1 %while.15 = (s32[]{:T(128)}, f32[512,4]{0,1:T(4,128)S(1)}, f32[512,4]{0,1:T(4,128)S(1)}, f32[512,4,192]{0,2,1:T(8,128)S(1)}, bf16[16,512,128]{2,1,0:T(8,128)(2,1...) while((s32[]{:T(128)}, f32[512,4]{0,1:T(4,128)S(1)}, ...), condition=%wide.region_4.5_spmd.clone, body=%wide.region_1.4_spmd.clone.sunk | while | flops 680667136 | bytes 33490052 | solution.py:55
  270.7 3.8 bitcast_reduce_fusion.2
  280.2 3.8 bitcast_reduce_fusion.2
  289.6 3.8 bitcast_reduce_fusion.2
  299.1 3.8 bitcast_reduce_fusion.2
  308.5 3.8 bitcast_reduce_fusion.2
  318.0 3.8 bitcast_reduce_fusion.2
  327.4 3.8 bitcast_reduce_fusion.2
  336.8 3.8 bitcast_reduce_fusion.2
  366.6 58.8 %psum.21 = bf16[32,768]{1,0:T(8,128)(2,1)S(1)} all-reduce(bf16[32,768]{1,0:T(8,128)(2,1)S(1)} %convolution_convert_fusion.4), channel_id=1, replica_groups=mesh['seq'=16,'batch'=16] {'seq'}, use_global_device_ids=true, to_apply=%region_7.8 | all-reduce | flops 24576 | bytes 98304 | tf_op jit(solution)/shard_map/psum | solution.py:124
  427.9 30.3 %all_to_all.10 = bf16[16,4,384]{2,1,0:T(4,128)(2,1)S(1)} all-to-all(bf16[16,4,384]{2,1,0:T(4,128)(2,1)S(1)} %copy.53), channel_id=1, replica_groups=mesh['seq'=16,'batch'=16] {'batch'}, dimensions={0} | all-to-all | bytes 98304 | tf_op jit(solution)/shard_map/all_to_all | solution.py:148
  458.9 8.7 %all_to_all.11 = bf16[16,4,384]{2,1,0:T(4,128)(2,1)S(1)} all-to-all(bf16[16,4,384]{2,1,0:T(4,128)(2,1)S(1)} %fusion.35), channel_id=1, replica_groups=mesh['seq'=16,'batch'=16] {'batch'}, dimensions={0} | all-to-all | bytes 98304 | tf_op jit(solution)/shard_map/all_to_all | solution.py:153
  468.5 4.0 convolution_convert_fusion
  476.0 27.0 %psum.23 = bf16[2,384]{1,0:T(2,128)(2,1)S(1)} all-reduce(bf16[2,384]{1,0:T(2,128)(2,1)S(1)} %fusion.36), channel_id=1, replica_groups=mesh['seq'=16,'batch'=16] {'batch'}, use_global_device_ids=true, to_apply=%region_11.12 | all-reduce | flops 768 | bytes 3072 | tf_op jit(solution)/shard_map/psum | solution.py:173
  503.5 87.8 %all-reduce.2.cloned.1.call-done = bf16[768,2,384]{2,0,1:T(8,128)(2,1)} async-done(((bf16[768,2,384]{2,0,1:T(8,128)(2,1)}), bf16[768,2,384]{2,0,1:T(8,128)(2,1)}) %all-reduce.2.cloned.1.call-update) | async-done | bytes 1179664 | tf_op jit(solution)/shard_map/psum | solution.py:172
  591.4 3.9 copy.54
  (208 shorter events, 143.6 us)
Async XLA Ops:
  7.2 25.6 %copy-start = (bf16[1536,512]{1,0:T(8,128)(2,1)S(1)}, bf16[1536,512]{1,0:T(8,128)(2,1)}, u32[]{:S(2)}) copy-start(bf16[1536,512]{1,0:T(8,128)(2,1)} %param.17) | copy-start | bytes 4718596
  7.2 17.7 %copy-start.3 = (bf16[1,512,1536]{2,1,0:T(8,128)(2,1)S(1)}, bf16[1,512,1536]{2,1,0:T(8,128)(2,1)}, u32[]{:S(2)}) copy-start(bf16[1,512,1536]{2,1,0:T(8,128)(2,1)} %param.14) | copy-start | bytes 4718596
  7.2 108.7 %all-gather.3.cloned.1.call-start = ((), (), s32[]{:S(2)}) async-start(), calls=%async_computation.2 | async-start | bytes 2228224 | tf_op jit(solution)/shard_map/all_gather | solution.py:100
  8.6 12.1 %collective-permute-start = (bf16[128,1536]{1,0:T(8,128)(2,1)S(1)}, bf16[128,1536]{1,0:T(8,128)(2,1)S(1)}, u32[]{:S(2)}, u32[]{:S(2)}) collective-permute-start(bf16[128,1536]{1,0:T(8,128)(2,1)S(1)} %get-tuple-element.137), channel_id=1, source_target_pairs={{0,16},{16,32},{32,48},{48,64},{64,80},{80,96},{96,112},{112,128},... | collective-permute-start | bytes 1179656 | tf_op jit(solution)/shard_map/ppermute | solution.py:20
  13.0 11.9 %collective-permute-start.1 = (bf16[128,1536]{1,0:T(8,128)(2,1)S(1)}, bf16[128,1536]{1,0:T(8,128)(2,1)S(1)}, u32[]{:S(2)}, u32[]{:S(2)}) collective-permute-start(bf16[128,1536]{1,0:T(8,128)(2,1)S(1)} %get-tuple-element.138), channel_id=1, source_target_pairs={{16,0},{32,16},{48,32},{64,48},{80,64},{96,80},{112,96},{128,112},... | collective-permute-start | bytes 1179656 | tf_op jit(solution)/shard_map/ppermute | solution.py:23
  24.9 3.8 copy-start.7
  24.9 3.8 copy-start.18
  30.2 180.0 %all-gather.5.cloned.1.call-start = ((), (), s32[]{:S(2)}) async-start(), calls=%async_computation.3 | async-start | bytes 3342336 | tf_op jit(solution)/shard_map/all_gather | solution.py:101
  30.9 560.5 %all-reduce.2.cloned.1.call-start = ((), (), s32[]{:S(2)}) async-start(), calls=%async_computation.4 | async-start | bytes 2359296 | tf_op jit(solution)/shard_map/psum | solution.py:172
  217.8 3.4 copy-start.1
  227.2 3.4 copy-start.1
  236.7 3.4 copy-start.1
  246.1 3.4 copy-start.1
  331.2 3.4 copy-start.1
  340.6 3.4 copy-start.1
  350.1 3.4 copy-start.1
  359.5 3.4 copy-start.1
  365.2 60.2 %copy-start.19 = (f32[2,384]{1,0:T(2,128)S(1)}, f32[2,384]{1,0:T(2,128)}, u32[]{:S(2)}) copy-start(f32[2,384]{1,0:T(2,128)} %param.20) | copy-start | bytes 9220
  365.4 62.1 %copy-start.22 = (pred[32]{0:T(512)(128)(4,1)S(1)}, pred[32]{0:T(512)(128)(4,1)}, u32[]{:S(2)}) copy-start(pred[32]{0:T(512)(128)(4,1)} %get-tuple-element.142) | copy-start | bytes 100
  365.4 62.1 %copy-start.23 = (s32[32]{0:T(128)S(1)}, s32[32]{0:T(128)}, u32[]{:S(2)}) copy-start(s32[32]{0:T(128)} %multiply_add_fusion.1) | copy-start | bytes 388
  365.4 93.4 %copy-start.15 = (f32[1,16,4,384]{3,2,1,0:T(4,128)S(1)}, f32[1,16,4,384]{3,2,1,0:T(4,128)}, u32[]{:S(2)}) copy-start(f32[1,16,4,384]{3,2,1,0:T(4,128)} %param.25) | copy-start | bytes 294916
  425.4 42.4 %copy-start.14 = (bf16[32,768]{1,0:T(8,128)(2,1)}, bf16[32,768]{1,0:T(8,128)(2,1)S(1)}, u32[]{:S(2)}) copy-start(bf16[32,768]{1,0:T(8,128)(2,1)S(1)} %psum.21) | copy-start | bytes 147460
  425.4 47.1 %copy-start.6 = (bf16[768,2,384]{2,1,0:T(2,128)(2,1)S(1)}, bf16[768,2,384]{2,1,0:T(2,128)(2,1)}, u32[]{:S(2)}) copy-start(bf16[768,2,384]{2,1,0:T(2,128)(2,1)} %param.19) | copy-start | bytes 3538948
  468.4 4.3 copy-start.5
  (20 other events, 51.5 us)
Sparse Core Ops, SparseCore 0:
  30.3 85.5 all-gather.2
  118.4 91.7 all-gather.4
  472.6 118.7 all-reduce.1
where the time goes:
time: 603 us; the launch traced here: 602 us
  waiting for transfers between devices  265 us (44%)
  blocking collectives  125 us (21%)
  matrix products  108 us (18%)
  other arithmetic  54.5 us (9%)
  local copies, waits for them, and re-layouts  28.9 us (5%)
  between operations  14.1 us (2%)
    all_gather x1, waiting for transfers between devices, local(): lax.all_gather(value_rows, 'seq', axis=0, tiled=True)  90.2 us
    psum x1, waiting for transfers between devices, local(): lax.psum(window_head.astype(jnp.bfloat16), 'batch').astype(jnp.float32)  87.8 us
    all_gather x1, waiting for transfers between devices, local(): lax.all_gather(key_rows, 'seq', axis=0, tiled=True)  77.2 us
    dot_general x16, matrix products, one_block(): jnp.einsum('qhd,kd->qhk', query_rows, key_block, preferred_element_type=j...  60 us
    psum x1, blocking collectives, local(): lax.psum(partial_pool.astype(jnp.bfloat16), 'seq').astype(jnp.float32)  58.8 us
    reduce_sum x16, other arithmetic, one_block(): running_sum = running_sum * shrink + jnp.sum(weights, axis=-1)  48.9 us
    dot_general x16, matrix products, one_block(): jnp.einsum('qhk,kd->qhd', weights.astype(jnp.bfloat16), value_block, pref...  35.4 us
    all_to_all x1, blocking collectives, local(): lax.all_to_all(outgoing.astype(jnp.bfloat16), 'batch', split_axis=0, conc...  30.3 us
  transfers between devices with their start and end apart: 5, of which 5 were waited for; matrix products, arithmetic and copies ran while one was open for 3% of the time, Pallas kernels for 0%

commit v1 on v0

--- a/solution.py
+++ b/solution.py
@@ -98,7 +98,9 @@
         start_state,
         (
             lax.all_gather(key_rows, "seq", axis=0, tiled=True),
-            lax.all_gather(value_rows, "seq", axis=0, tiled=True),
+            jnp.concatenate(
+                lax.all_to_all(jnp.stack([value_rows] * lax.axis_size("seq")), "seq", 0, 0), axis=0
+            ),
         ),
     )
     hidden_width = HEADS * DV

time: 603 us -> 554 us (0.919)
  waiting for transfers between devices: 265 us -> 206 us
  starting transfers between devices: 5.81 us -> 16.4 us
    all_gather x1 -> x0, waiting for transfers between devices: 90.2 us -> none  [local(): lax.all_gather(value_rows, 'seq', axis=0, tiled=True)]
    all_gather x1, waiting for transfers between devices: 77.2 us -> 108 us  [local(): lax.all_gather(key_rows, 'seq', axis=0, tiled=True)]
    all_to_all x0 -> x1, starting transfers between devices: none -> 10.6 us  [local(): lax.all_to_all(jnp.stack([value_rows] * lax.axis_size('seq')), 'seq', 0, 0)]
  transfers between devices with their start and end apart: 5 -> 5, of which waited for: 5 -> 4; matrix products, arithmetic and copies ran while one was open for 3% -> 3% of each run, Pallas kernels for 0% -> 0%
where the time goes in v1:
time: 554 us; the launch traced here: 552 us
  waiting for transfers between devices  206 us (37%)
  blocking collectives  125 us (23%)
  matrix products  111 us (20%)
  other arithmetic  54.5 us (10%)
  local copies, waits for them, and re-layouts  25.3 us (5%)
  starting transfers between devices  16.4 us (3%)
  between operations  14.4 us (3%)
    all_gather x1, waiting for transfers between devices, local(): lax.all_gather(key_rows, 'seq', axis=0, tiled=True)  108 us
    psum x1, waiting for transfers between devices, local(): lax.psum(window_head.astype(jnp.bfloat16), 'batch').astype(jnp.float32)  87.9 us
    dot_general x16, matrix products, one_block(): jnp.einsum('qhd,kd->qhk', query_rows, key_block, preferred_element_type=j...  62.2 us
    psum x1, blocking collectives, local(): lax.psum(partial_pool.astype(jnp.bfloat16), 'seq').astype(jnp.float32)  59.6 us
    reduce_sum x16, other arithmetic, one_block(): running_sum = running_sum * shrink + jnp.sum(weights, axis=-1)  48.9 us
    dot_general x16, matrix products, one_block(): jnp.einsum('qhk,kd->qhd', weights.astype(jnp.bfloat16), value_block, pref...  35.4 us
    all_to_all x1, blocking collectives, local(): lax.all_to_all(outgoing.astype(jnp.bfloat16), 'batch', split_axis=0, conc...  29.6 us
    psum x1, blocking collectives, local(): lax.psum(window_bias.astype(jnp.bfloat16), 'batch').astype(jnp.float32)  27 us
  transfers between devices with their start and end apart: 5, of which 4 were waited for; matrix products, arithmetic and copies ran while one was open for 3% of the time, Pallas kernels for 0%

profile of v1, /device:TPU:1, one launch (start us, length us, event | category | flops | bytes accessed | tf_op | source)
XLA Modules:
  0.0 552.2 jit_solution(15619738844478998822)
XLA Ops:
  8.5 4.4 collective-permute-start
  15.3 5.3 collective-permute-done
  20.7 4.2 collective-permute-done.1
  30.6 10.6 %all-to-all-start = ((bf16[16,512,192]{1,2,0:T(8,128)(2,1)}), bf16[16,512,192]{1,2,0:T(8,128)(2,1)}, u32[]{:S(2)}, u32[]{:S(2)}) async-start(bf16[16,512,192]{1,2,0:T(8,128)(2,1)} %stack.8), calls=%async_computation | async-start | bytes 6291456 | tf_op jit(solution)/shard_map/all_to_all | solution.py:102
  49.6 108.2 %all-gather.2.cloned.1.call-done = bf16[8192,128]{0,1:T(8,128)(2,1)} async-done(((bf16[512,128]{0,1:T(8,128)(2,1)}), bf16[8192,128]{0,1:T(8,128)(2,1)}) %all-gather.2.cloned.1.call-update) | async-done | bytes 2097168 | tf_op jit(solution)/shard_map/all_gather | solution.py:100
  157.8 4.1 copy.52
  161.9 153.3 %while.15 = (s32[]{:T(128)}, f32[512,4]{0,1:T(4,128)S(1)}, f32[512,4]{0,1:T(4,128)S(1)}, f32[512,4,192]{0,2,1:T(8,128)S(1)}, bf16[16,512,128]{2,1,0:T(8,128)(2,1...) while((s32[]{:T(128)}, f32[512,4]{0,1:T(4,128)S(1)}, ...), condition=%wide.region_4.5_spmd.clone, body=%wide.region_1.4_spmd.clone.sunk | while | flops 680667136 | bytes 33490052 | solution.py:55
  181.0 3.9 bitcast_reduce_fusion.2
  190.6 3.9 bitcast_reduce_fusion.2
  200.2 3.9 bitcast_reduce_fusion.2
  219.4 3.9 bitcast_reduce_fusion.2
  238.5 3.9 bitcast_reduce_fusion.2
  257.7 3.9 bitcast_reduce_fusion.2
  267.3 3.9 bitcast_reduce_fusion.2
  276.9 3.9 bitcast_reduce_fusion.2
  286.5 3.9 bitcast_reduce_fusion.2
  296.0 3.9 bitcast_reduce_fusion.2
  316.6 59.6 %psum.21 = bf16[32,768]{1,0:T(8,128)(2,1)S(1)} all-reduce(bf16[32,768]{1,0:T(8,128)(2,1)S(1)} %convolution_convert_fusion.4), channel_id=1, replica_groups=mesh['seq'=16,'batch'=16] {'seq'}, use_global_device_ids=true, to_apply=%region_7.8 | all-reduce | flops 24576 | bytes 98304 | tf_op jit(solution)/shard_map/psum | solution.py:126
  378.7 29.6 %all_to_all.15 = bf16[16,4,384]{2,1,0:T(4,128)(2,1)S(1)} all-to-all(bf16[16,4,384]{2,1,0:T(4,128)(2,1)S(1)} %copy.49), channel_id=1, replica_groups=mesh['seq'=16,'batch'=16] {'batch'}, dimensions={0} | all-to-all | bytes 98304 | tf_op jit(solution)/shard_map/all_to_all | solution.py:150
  409.0 8.7 %all_to_all.16 = bf16[16,4,384]{2,1,0:T(4,128)(2,1)S(1)} all-to-all(bf16[16,4,384]{2,1,0:T(4,128)(2,1)S(1)} %fusion.35), channel_id=1, replica_groups=mesh['seq'=16,'batch'=16] {'batch'}, dimensions={0} | all-to-all | bytes 98304 | tf_op jit(solution)/shard_map/all_to_all | solution.py:155
  418.5 4.0 convolution_convert_fusion
  426.1 27.0 %psum.23 = bf16[2,384]{1,0:T(2,128)(2,1)S(1)} all-reduce(bf16[2,384]{1,0:T(2,128)(2,1)S(1)} %fusion.36), channel_id=1, replica_groups=mesh['seq'=16,'batch'=16] {'batch'}, use_global_device_ids=true, to_apply=%region_11.12 | all-reduce | flops 768 | bytes 3072 | tf_op jit(solution)/shard_map/psum | solution.py:175
  453.6 87.9 %all-reduce.2.cloned.1.call-done = bf16[768,2,384]{2,0,1:T(8,128)(2,1)} async-done(((bf16[768,2,384]{2,0,1:T(8,128)(2,1)}), bf16[768,2,384]{2,0,1:T(8,128)(2,1)}) %all-reduce.2.cloned.1.call-update) | async-done | bytes 1179664 | tf_op jit(solution)/shard_map/psum | solution.py:174
  541.5 3.9 copy.50
  (207 shorter events, 141.0 us)
Async XLA Ops:
  7.2 36.6 %copy-start = (bf16[1536,512]{1,0:T(8,128)(2,1)S(1)}, bf16[1536,512]{1,0:T(8,128)(2,1)}, u32[]{:S(2)}) copy-start(bf16[1536,512]{1,0:T(8,128)(2,1)} %param.17) | copy-start | bytes 4718596
  7.2 17.6 %copy-start.3 = (bf16[1,512,1536]{2,1,0:T(8,128)(2,1)S(1)}, bf16[1,512,1536]{2,1,0:T(8,128)(2,1)}, u32[]{:S(2)}) copy-start(bf16[1,512,1536]{2,1,0:T(8,128)(2,1)} %param.14) | copy-start | bytes 4718596
  8.5 12.1 %collective-permute-start = (bf16[128,1536]{1,0:T(8,128)(2,1)S(1)}, bf16[128,1536]{1,0:T(8,128)(2,1)S(1)}, u32[]{:S(2)}, u32[]{:S(2)}) collective-permute-start(bf16[128,1536]{1,0:T(8,128)(2,1)S(1)} %get-tuple-element.137), channel_id=1, source_target_pairs={{0,16},{16,32},{32,48},{48,64},{64,80},{80,96},{96,112},{112,128},... | collective-permute-start | bytes 1179656 | tf_op jit(solution)/shard_map/ppermute | solution.py:20
  12.9 11.9 %collective-permute-start.1 = (bf16[128,1536]{1,0:T(8,128)(2,1)S(1)}, bf16[128,1536]{1,0:T(8,128)(2,1)S(1)}, u32[]{:S(2)}, u32[]{:S(2)}) collective-permute-start(bf16[128,1536]{1,0:T(8,128)(2,1)S(1)} %get-tuple-element.138), channel_id=1, source_target_pairs={{16,0},{32,16},{48,32},{64,48},{80,64},{96,80},{112,96},{128,112},... | collective-permute-start | bytes 1179656 | tf_op jit(solution)/shard_map/ppermute | solution.py:23
  30.6 11.4 %copy-start.17 = (s32[1,32,8]{1,2,0:T(8,128)S(1)}, s32[1,32,8]{1,2,0:T(8,128)}, u32[]{:S(2)}) copy-start(s32[1,32,8]{1,2,0:T(8,128)} %param.21) | copy-start | bytes 3076
  30.6 11.5 %copy-start.16 = (s32[1,32,8]{1,2,0:T(8,128)S(1)}, s32[1,32,8]{1,2,0:T(8,128)}, u32[]{:S(2)}) copy-start(s32[1,32,8]{1,2,0:T(8,128)} %param.22) | copy-start | bytes 3076
  30.6 11.6 %copy-start.21 = (s32[1,32,1]{1,2,0:T(1,128)S(1)}, s32[1,32,1]{1,2,0:T(1,128)}, u32[]{:S(2)}) copy-start(s32[1,32,1]{1,2,0:T(1,128)} %param.24) | copy-start | bytes 388
  30.6 12.1 %copy-start.20 = (s32[1,32]{1,0:T(1,128)S(1)}, s32[1,32]{1,0:T(1,128)}, u32[]{:S(2)}) copy-start(s32[1,32]{1,0:T(1,128)} %param.23) | copy-start | bytes 388
  30.6 131.3 %all-to-all-start = ((bf16[16,512,192]{1,2,0:T(8,128)(2,1)}), bf16[16,512,192]{1,2,0:T(8,128)(2,1)}, u32[]{:S(2)}, u32[]{:S(2)}) async-start(bf16[16,512,192]{1,2,0:T(8,128)(2,1)} %stack.8), calls=%async_computation | async-start | bytes 6291456 | tf_op jit(solution)/shard_map/all_to_all | solution.py:102
  41.2 116.6 %all-gather.2.cloned.1.call-start = ((), (), s32[]{:S(2)}) async-start(), calls=%async_computation.3 | async-start | bytes 2228224 | tf_op jit(solution)/shard_map/all_gather | solution.py:100
  41.9 499.6 %all-reduce.2.cloned.1.call-start = ((), (), s32[]{:S(2)}) async-start(), calls=%async_computation.4 | async-start | bytes 2359296 | tf_op jit(solution)/shard_map/psum | solution.py:174
  165.8 3.4 copy-start.1
  175.3 3.4 copy-start.1
  223.3 3.4 copy-start.1
  242.4 3.4 copy-start.1
  252.0 3.4 copy-start.1
  271.2 3.4 copy-start.1
  315.2 61.1 %copy-start.19 = (f32[2,384]{1,0:T(2,128)S(1)}, f32[2,384]{1,0:T(2,128)}, u32[]{:S(2)}) copy-start(f32[2,384]{1,0:T(2,128)} %param.20) | copy-start | bytes 9220
  315.4 63.0 %copy-start.22 = (pred[32]{0:T(512)(128)(4,1)S(1)}, pred[32]{0:T(512)(128)(4,1)}, u32[]{:S(2)}) copy-start(pred[32]{0:T(512)(128)(4,1)} %get-tuple-element.142) | copy-start | bytes 100
  315.4 62.9 %copy-start.23 = (s32[32]{0:T(128)S(1)}, s32[32]{0:T(128)}, u32[]{:S(2)}) copy-start(s32[32]{0:T(128)} %multiply_add_fusion.1) | copy-start | bytes 388
  315.5 93.5 %copy-start.15 = (f32[1,16,4,384]{3,2,1,0:T(4,128)S(1)}, f32[1,16,4,384]{3,2,1,0:T(4,128)}, u32[]{:S(2)}) copy-start(f32[1,16,4,384]{3,2,1,0:T(4,128)} %param.25) | copy-start | bytes 294916
  376.2 41.7 %copy-start.14 = (bf16[32,768]{1,0:T(8,128)(2,1)}, bf16[32,768]{1,0:T(8,128)(2,1)S(1)}, u32[]{:S(2)}) copy-start(bf16[32,768]{1,0:T(8,128)(2,1)S(1)} %psum.21) | copy-start | bytes 147460
  376.3 46.3 %copy-start.6 = (bf16[768,2,384]{2,1,0:T(2,128)(2,1)S(1)}, bf16[768,2,384]{2,1,0:T(2,128)(2,1)}, u32[]{:S(2)}) copy-start(bf16[768,2,384]{2,1,0:T(2,128)(2,1)} %param.19) | copy-start | bytes 3538948
  418.5 4.3 copy-start.5
  (20 other events, 52.0 us)
Sparse Core Ops, SparseCore 0:
  45.1 112.7 all-gather.1
  422.7 118.7 all-reduce.1
